TPU v7x, 32 devices: a whole 2x2x4 slice. The times are simulated.
32 devices in a mesh: slab: 2 (over y), sec: 8 (over z, x), tile: 2 (over core).
Axes of the slice: x: 2, y: 2, z: 4, core: 2. Of those that a mesh axis runs over, the one named last changes fastest.
Arguments:
- image: bfloat16 [16, 128, 4096], P(('slab', 'sec'), 'tile'), parts along dimension 0, may hold values from -6 to 6
- keyframe: int32 [16], P(('slab', 'sec')), parts along dimension 0, may hold values from 0 to 7, as said below
- offsets: int32 [16, 64], P(('slab', 'sec')), parts along dimension 0, may hold values from -16 to 16
Outputs:
- warped: bfloat16 [16, 128, 4096], P(('slab', 'sec'), 'tile'), parts along dimension 0
- field: float32 [16, 2, 2, 64], P(('slab', 'sec'), None, 'tile'), parts along dimension 0
- pyramid: float32 [16, 16, 512], P(('slab', 'sec'), 'tile'), parts along dimension 0
There are 2 independent parts, one for each index of `slab`. A program takes and returns all parts, laid end to end along the dimension named above; each array names one. Nothing has to cross between parts.
Inputs may be any that keep to these rules, and one draw needn't show every extreme that they name: Sections 0, 3 and 7 are keyframes and section 4 is not; keyframe[s] is the largest keyframe index at or before s, and a keyframe is its own keyframe.
All inputs are finite; a program needn't handle non-finite values.
Results may differ from a plain program's by a relative error of at most 0.0033.
Values may be sent and summed in bfloat16 or wider, within the bound.
A program may use at most 64 MiB of HBM per device.

v0:
```python
import jax
import jax.numpy as jnp
from jax import lax
from jax.sharding import PartitionSpec as P

PATCH = 64
KCOEF = 8
WIN = 8


HIGH = lax.Precision.HIGHEST
REG = 4.0


def with_halo(value, sides, width):
    for axis, dim in sides:
        size, length = (lax.axis_size(axis), value.shape[dim])
        up = [(i, (i + 1) % size) for i in range(size - 1)]
        down = [(j, i) for i, j in up]
        last = lax.slice_in_dim(value, length - width, length, axis=dim)
        leading = lax.slice_in_dim(value, 0, width, axis=dim)
        before = lax.ppermute(last, axis, up)
        after = lax.ppermute(leading, axis, down)
        value = jnp.concatenate([before, value, after], axis=dim)
    return value


def from_behind(value, axis, steps):
    count = lax.axis_size(axis)
    leading, last = (max(0, -steps), min(count, count - steps))
    return lax.ppermute(value, axis, [(source, source + steps) for source in range(leading, last)])


def cosine_table():
    index = jnp.arange(PATCH, dtype=jnp.float32)
    order = jnp.arange(KCOEF, dtype=jnp.float32)
    table = jnp.sqrt(2.0 / PATCH) * jnp.cos(
        jnp.pi * (index[None, :] + 0.5) * order[:, None] / PATCH
    )
    scale = jnp.where(order == 0, jnp.sqrt(0.5), 1.0)
    return table * scale[:, None]


def describe(field, table):
    rows, cols = field.shape
    first = jnp.einsum(
        "rtj,bj->rtb", field.reshape(rows, cols // PATCH, PATCH), table, precision=HIGH
    )
    first = first.reshape(rows // PATCH, PATCH, cols // PATCH * KCOEF)
    second = jnp.einsum("pic,ai->pac", first, table, precision=HIGH)
    return second.reshape(rows // PATCH * KCOEF, cols // PATCH * KCOEF)


def patch_sums(values):
    rows, cols = values.shape
    return values.reshape(rows // KCOEF, KCOEF, cols // KCOEF, KCOEF).sum(axis=(1, 3))


def displacement(desc, d_col, d_row, refer):
    diff = refer.astype(jnp.float32) - desc.astype(jnp.float32)
    gxx = patch_sums(d_col * d_col) + REG
    gxy = patch_sums(d_col * d_row)
    gyy = patch_sums(d_row * d_row) + REG
    b_col = patch_sums(d_col * diff)
    b_row = patch_sums(d_row * diff)
    det = gxx * gyy - gxy * gxy
    return ((gyy * b_col - gxy * b_row) / det, (gxx * b_row - gxy * b_col) / det)


def taps(shift):
    return (
        -shift * (shift - 1.0) * (shift - 2.0) / 6.0,
        (shift + 1.0) * (shift - 1.0) * (shift - 2.0) / 2.0,
        -(shift + 1.0) * shift * (shift - 2.0) / 2.0,
        (shift + 1.0) * shift * (shift - 1.0) / 6.0,
    )


def warp(extended, u_col, u_row, offs):
    rows = extended.shape[0] - 4
    cols = extended.shape[1]
    prow, pcol = (rows // PATCH, cols // PATCH)
    vert = jnp.zeros((prow, PATCH, pcol, PATCH), jnp.float32)
    for k, weight in enumerate(taps(u_row)):
        part = extended[1 + k : 1 + k + rows].reshape(prow, PATCH, pcol, PATCH)
        vert = vert + weight[:, None, :, None] * part
    padded = jnp.pad(vert, ((0, 0), (0, 0), (1, 1), (0, 0)))
    window = jnp.concatenate(
        [padded[:, :, 0:pcol], padded[:, :, 1 : pcol + 1], padded[:, :, 2 : pcol + 2]], axis=-1
    )
    widx = jnp.arange(3 * PATCH, dtype=jnp.int32)[None, None, :, None]
    jidx = jnp.arange(PATCH, dtype=jnp.int32)[None, None, None, :]
    base = jidx + PATCH + offs[None, :, None, None]
    matrix = jnp.zeros((prow, pcol, 3 * PATCH, PATCH), jnp.float32)
    for k, weight in enumerate(taps(u_col)):
        matrix = matrix + weight[:, :, None, None] * (widx == base + (k - 1)).astype(jnp.float32)
    out = jnp.einsum("pitw,ptwj->pitj", window, matrix, precision=HIGH)
    return out.reshape(rows, cols)


def body(image, keyframe, offsets):
    table = cosine_table()
    section = image[0]
    rims = with_halo(section, (("tile", 0),), 2)
    extended = rims.astype(jnp.float32)
    sides = jnp.pad(extended, ((0, 0), (1, 1)))
    center = extended[2:-2]
    g_col = (sides[2:-2, 2:] - sides[2:-2, :-2]) * 0.5
    g_row = (extended[3:-1] - extended[1:-3]) * 0.5
    desc = describe(center, table).astype(jnp.bfloat16)
    d_col = describe(g_col, table)
    d_row = describe(g_row, table)
    everyone = lax.all_gather(desc[None], "sec", axis=0, tiled=True)
    keyref = lax.dynamic_index_in_dim(everyone, keyframe[0], 0, keepdims=False)
    predref = from_behind(desc, "sec", 1)
    kc, kr = displacement(desc, d_col, d_row, keyref)
    pc, pr = displacement(desc, d_col, d_row, predref)
    u_col = 0.5 * (kc + pc)
    u_row = 0.5 * (kr + pr)
    out = warp(extended, u_col, u_row, offsets[0])
    rows, cols = out.shape
    block = out.reshape(rows // 8, 8, cols // 8, 8).sum(axis=(1, 3))
    total = block
    for back in range(1, WIN):
        total = total + from_behind(block, "sec", back)
    pyramid = total / 512.0
    return (out.astype(jnp.bfloat16)[None], jnp.stack([u_col, u_row])[None], pyramid[None])


def solution(mesh):
    return jax.shard_map(
        body,
        mesh=mesh,
        in_specs=(P(("slab", "sec"), "tile", None), P(("slab", "sec")), P(("slab", "sec"), None)),
        out_specs=(
            P(("slab", "sec"), "tile", None),
            P(("slab", "sec"), None, "tile", None),
            P(("slab", "sec"), "tile", None),
        ),
        check_vma=False,
    )
```

profile of v0, /device:TPU:0, one launch (start us, length us, event | category | flops | bytes accessed | tf_op | source)
XLA Modules:
  0.0 136.4 jit_solution(14255106977008558467)
XLA Ops:
  0.7 1.0 slice_bitcast_fusion.1
  1.6 2.4 %collective-permute-start = (bf16[2,4096]{1,0:T(2,128)(2,1)S(1)}, bf16[2,4096]{1,0:T(2,128)(2,1)S(1)}, u32[]{:S(2)}, u32[]{:S(2)}) collective-permute-start(bf16[2,4096]{1,0:T(2,128)(2,1)S(1)} %get-tuple-element.28), channel_id=1, source_target_pairs={{0,1},{2,3},{4,5},{6,7},{8,9},{10,11},{12,13},{14,15},{16,17},{18,... | collective-permute-start | bytes 49160 | tf_op jit(solution)/shard_map/ppermute | solution.py:22
  4.0 1.3 collective-permute-start.1
  5.3 2.1 %reshape.809 = bf16[64,64,64]{2,1,0:T(8,128)(2,1)S(1)} reshape(bf16[1,64,4096]{2,1,0:T(8,128)(2,1)} %param.3) | data formatting | bytes 1048576 | tf_op jit(solution)/shard_map/reshape | solution.py:47
  7.4 2.5 %convolution_bitcast_fusion = f32[64,64,8]{1,2,0:T(8,128)S(1)} fusion(bf16[64,64,64]{2,1,0:T(8,128)(2,1)S(1)} %reshape.809, f32[8]{0:T(128)S(1)} %fusion.57, f32[64]{0:T(128)S(1)} %add_multiply_fusion.2), kind=kOutput, calls=%fused_computation.36 | convolution fusion | flops 25167360 | bytes 655648 | tf_op jit(solution)/shard_map/rtj,bj->rtb/dot_general | solution.py:46
  10.5 4.8 %collective-permute-start.2 = (bf16[8,512]{1,0:T(8,128)(2,1)S(1)}, bf16[8,512]{1,0:T(8,128)(2,1)}, u32[]{:S(2)}, u32[]{:S(2)}) collective-permute-start(bf16[8,512]{1,0:T(8,128)(2,1)S(1)} %convolution_convert_fusion), channel_id=1, source_target_pairs={{0,2},{2,4},{4,6},{6,8},{8,10},{10,12},{12,14},{1,3},{3,5},{5,7},{... | collective-permute-start | bytes 24584 | tf_op jit(solution)/shard_map/ppermute | solution.py:31
  16.0 0.7 add_add_fusion.2
  16.7 30.7 %all-gather = bf16[64,512]{1,0:T(8,128)(2,1)S(1)} all-gather(bf16[8,512]{1,0:T(8,128)(2,1)S(1)} %convolution_convert_fusion), channel_id=2, replica_groups=mesh['slab'=2,'sec'=8,'tile'=2] {'sec'}, dimensions={0}, use_global_device_ids=true | all-gather | bytes 73728 | tf_op jit(solution)/shard_map/all_gather | solution.py:113
  47.6 3.0 %fusion.28 = (f32[64,4096]{1,0:T(8,128)}, f32[64,4096]{1,0:T(8,128)}, f32[64,4096]{1,0:T(8,128)}, f32[64,4096]{1,0:T(8,128)}, f32[64,4096]{1,0:T(8,128)}, /*index=5*/f32[64,4096]{1,0:T(8,128)S(1)}) fusion(f32[68,4096]{1,0:T(8,128)S(1)} %maximum_convert_fusion), kind=kLoop, calls=%fused_computation.41 | loop fusion | flops 1048576 | bytes 11665408 | tf_op jit(solution)/shard_map/mul | solution.py:108
  50.6 2.0 %reshape.807 = f32[64,64,64]{2,1,0:T(8,128)S(1)} reshape(f32[64,4096]{1,0:T(8,128)} %get-tuple-element.22) | data formatting | bytes 2097152 | tf_op jit(solution)/shard_map/reshape | solution.py:47
  52.6 5.0 %fusion.35 = f32[64,64,8]{1,2,0:T(8,128)S(1)} fusion(f32[64,64,64]{2,1,0:T(8,128)S(1)} %reshape.807, f32[8]{0:T(128)S(1)} %fusion.57, f32[64]{0:T(128)S(1)} %add_multiply_fusion.2), kind=kOutput, calls=%fused_computation.66 | convolution fusion | flops 25167360 | bytes 1179936 | tf_op jit(solution)/shard_map/rtj,bj->rtb/dot_general | solution.py:46
  57.5 0.9 copy.9
  58.4 2.0 %reshape.805 = f32[64,64,64]{2,1,0:T(8,128)S(1)} reshape(f32[64,4096]{1,0:T(8,128)} %get-tuple-element.23) | data formatting | bytes 2097152 | tf_op jit(solution)/shard_map/reshape | solution.py:47
  60.4 5.0 %fusion.37 = f32[64,64,8]{1,2,0:T(8,128)S(1)} fusion(f32[64,64,64]{2,1,0:T(8,128)S(1)} %reshape.805, f32[8]{0:T(128)S(1)} %fusion.57, f32[64]{0:T(128)S(1)} %add_multiply_fusion.2), kind=kOutput, calls=%fused_computation.68 | convolution fusion | flops 25167360 | bytes 1179936 | tf_op jit(solution)/shard_map/rtj,bj->rtb/dot_general | solution.py:46
  66.0 1.1 multiply_reduce_fusion.3
  68.5 2.0 %reshape.814 = f32[1,64,64,64]{3,2,1,0:T(8,128)S(1)} reshape(f32[64,4096]{1,0:T(8,128)} %get-tuple-element.24) | data formatting | bytes 2097152 | tf_op jit(solution)/shard_map/reshape | solution.py:85
  70.6 3.1 %reshape.812 = f32[1,64,64,64]{3,2,1,0:T(8,128)} reshape(f32[64,4096]{1,0:T(8,128)} %get-tuple-element.25) | data formatting | bytes 2097152 | tf_op jit(solution)/shard_map/reshape | solution.py:85
  73.7 3.1 %reshape.811 = f32[1,64,64,64]{3,2,1,0:T(8,128)} reshape(f32[64,4096]{1,0:T(8,128)} %get-tuple-element.26) | data formatting | bytes 2097152 | tf_op jit(solution)/shard_map/reshape | solution.py:85
  76.7 2.2 %reshape.813 = f32[1,64,64,64]{3,2,1,0:T(8,128)} reshape(f32[64,4096]{1,0:T(8,128)S(1)} %get-tuple-element.27) | data formatting | bytes 2097152 | tf_op jit(solution)/shard_map/reshape | solution.py:85
  78.9 10.6 %fusion.12 = f32[1,64,64,64]{3,1,2,0:T(8,128)S(1)} fusion(f32[1,64,64,64]{3,2,1,0:T(8,128)S(1)} %reshape.814, f32[1,64,64,64]{3,2,1,0:T(8,128)} %reshape.813, f32[1,64,64,64]{3,2,1,0:T(8,128)} %reshape.812, f32[1,64,64,64]{3,2,1,0:T(8,128)} %reshape.811, f32[64]{0:T(128)S(1)} %get-tuple-element.40, f32[64]{0:T(128)S(1)} %get-tuple-element.41, ...), kind=kLoop, calls=%fused_computation.18 | loop fusion | flops 1835008 | bytes 5243904 | tf_op jit(solution)/shard_map/add | solution.py:86
  90.3 10.7 %fusion.66 = (bf16[1,64,64,64]{1,3,2,0:T(8,128)(2,1)S(1)}, f32[1,64,64,64]{1,3,2,0:T(8,128)}) fusion(f32[1,64,64,64]{3,1,2,0:T(8,128)S(1)} %get-tuple-element.21, f32[1,64,64,64]{3,1,2,0:T(8,128)S(1)} %fusion.12, f32[1,64,64,64]{3,1,2,0:T(8,128)S(1)} %get-tuple-element.20, f32[64]{0:T(128)S(1)} %get-tuple-element.45, s32[64,64]{1,0:T(8,128)S(1)} %get-tuple-element.33, ...), kind=kOutput, calls=%fused_computation.117 | convolution fusion | flops 614465536 | bytes 4785152 | tf_op jit(solution)/shard_map/pitw,ptwj->pitj/dot_general | solution.py:97
  101.0 3.1 %copy.15 = f32[1,64,64,64]{3,2,1,0:T(8,128)S(1)} copy(f32[1,64,64,64]{1,3,2,0:T(8,128)} %get-tuple-element.43) | data formatting | bytes 2097152 | tf_op jit(solution)/shard_map/pitw,ptwj->pitj/transpose | solution.py:97
  104.1 8.4 %reshape_reshape.3 = f32[8,8,512,8]{3,2,1,0:T(8,128)} reshape(f32[1,64,64,64]{3,2,1,0:T(8,128)S(1)} %copy.15) | data formatting | bytes 2097152 | tf_op jit(solution)/shard_map/reshape;reshape | solution.py:122
  112.6 6.9 %reduce_sum.154 = f32[8,512]{1,0:T(8,128)S(1)} reduce(f32[8,8,512,8]{3,2,1,0:T(8,128)} %reshape_reshape.3, f32[]{:T(128)} %constant.47.clone.1), dimensions={1,3}, to_apply=%region_14.15 | reduce | flops 258048 | bytes 1064964 | tf_op jit(solution)/shard_map/reduce_sum | solution.py:122
  119.5 3.7 %collective-permute-start.9 = (f32[8,512]{1,0:T(8,128)S(1)}, f32[8,512]{1,0:T(8,128)S(1)}, u32[]{:S(2)}, u32[]{:S(2)}) collective-permute-start(f32[8,512]{1,0:T(8,128)S(1)} %reduce_sum.154), channel_id=1, source_target_pairs={{0,14},{1,15},{16,30},{17,31}} | collective-permute-start | bytes 49160 | tf_op jit(solution)/shard_map/ppermute | solution.py:31
  123.3 1.3 collective-permute-start.8
  124.6 1.3 collective-permute-start.7
  125.9 1.3 collective-permute-start.6
  127.2 2.5 %collective-permute-start.5 = (f32[8,512]{1,0:T(8,128)S(1)}, f32[8,512]{1,0:T(8,128)S(1)}, u32[]{:S(2)}, u32[]{:S(2)}) collective-permute-start(f32[8,512]{1,0:T(8,128)S(1)} %reduce_sum.154), channel_id=1, source_target_pairs={{0,6},{2,8},{4,10},{6,12},{8,14},{1,7},{3,9},{5,11},{7,13},{9,15},... | collective-permute-start | bytes 49160 | tf_op jit(solution)/shard_map/ppermute | solution.py:31
  129.6 1.3 collective-permute-start.4
  131.0 3.1 %collective-permute-start.3 = (f32[8,512]{1,0:T(8,128)S(1)}, f32[8,512]{1,0:T(8,128)S(1)}, u32[]{:S(2)}, u32[]{:S(2)}) collective-permute-start(f32[8,512]{1,0:T(8,128)S(1)} %reduce_sum.154), channel_id=1, source_target_pairs={{0,2},{2,4},{4,6},{6,8},{8,10},{10,12},{12,14},{1,3},{3,5},{5,7},{... | collective-permute-start | bytes 49160 | tf_op jit(solution)/shard_map/ppermute | solution.py:31
  134.6 1.1 copy.16
  (47 shorter events, 4.7 us)
Async XLA Ops:
  0.6 46.8 %copy-start = (bf16[1,64,4096]{2,1,0:T(8,128)(2,1)S(1)}, bf16[1,64,4096]{2,1,0:T(8,128)(2,1)}, u32[]{:S(2)}) copy-start(bf16[1,64,4096]{2,1,0:T(8,128)(2,1)} %param.3) | copy-start | bytes 1572868
  0.6 15.3 %copy-start.4 = (s32[1,64]{1,0:T(1,128)S(1)}, s32[1,64]{1,0:T(1,128)}, u32[]{:S(2)}) copy-start(s32[1,64]{1,0:T(1,128)} %param.5) | copy-start | bytes 772
  1.6 45.8 %collective-permute-start = (bf16[2,4096]{1,0:T(2,128)(2,1)S(1)}, bf16[2,4096]{1,0:T(2,128)(2,1)S(1)}, u32[]{:S(2)}, u32[]{:S(2)}) collective-permute-start(bf16[2,4096]{1,0:T(2,128)(2,1)S(1)} %get-tuple-element.28), channel_id=1, source_target_pairs={{0,1},{2,3},{4,5},{6,7},{8,9},{10,11},{12,13},{14,15},{16,17},{18,... | collective-permute-start | bytes 49160 | tf_op jit(solution)/shard_map/ppermute | solution.py:22
  4.0 43.4 %collective-permute-start.1 = (bf16[2,4096]{1,0:T(2,128)(2,1)S(1)}, bf16[2,4096]{1,0:T(2,128)(2,1)S(1)}, u32[]{:S(2)}, u32[]{:S(2)}) collective-permute-start(bf16[2,4096]{1,0:T(2,128)(2,1)S(1)} %get-tuple-element.29), channel_id=1, source_target_pairs={{1,0},{3,2},{5,4},{7,6},{9,8},{11,10},{13,12},{15,14},{17,16},{19,... | collective-permute-start | bytes 49160 | tf_op jit(solution)/shard_map/ppermute | solution.py:23
  10.5 55.5 %collective-permute-start.2 = (bf16[8,512]{1,0:T(8,128)(2,1)S(1)}, bf16[8,512]{1,0:T(8,128)(2,1)}, u32[]{:S(2)}, u32[]{:S(2)}) collective-permute-start(bf16[8,512]{1,0:T(8,128)(2,1)S(1)} %convolution_convert_fusion), channel_id=1, source_target_pairs={{0,2},{2,4},{4,6},{6,8},{8,10},{10,12},{12,14},{1,3},{3,5},{5,7},{... | collective-permute-start | bytes 24584 | tf_op jit(solution)/shard_map/ppermute | solution.py:31
  60.4 5.0 %copy-start.1 = (f32[64,64,8]{0,2,1:T(8,128)S(1)}, f32[64,64,8]{0,2,1:T(8,128)}, u32[]{:S(2)}) copy-start(f32[64,64,8]{0,2,1:T(8,128)} %copy.9) | copy-start | bytes 393220
  89.5 0.8 copy-start.2
  89.5 0.8 copy-start.3
  119.5 10.1 %collective-permute-start.9 = (f32[8,512]{1,0:T(8,128)S(1)}, f32[8,512]{1,0:T(8,128)S(1)}, u32[]{:S(2)}, u32[]{:S(2)}) collective-permute-start(f32[8,512]{1,0:T(8,128)S(1)} %reduce_sum.154), channel_id=1, source_target_pairs={{0,14},{1,15},{16,30},{17,31}} | collective-permute-start | bytes 49160 | tf_op jit(solution)/shard_map/ppermute | solution.py:31
  123.3 7.7 %collective-permute-start.8 = (f32[8,512]{1,0:T(8,128)S(1)}, f32[8,512]{1,0:T(8,128)S(1)}, u32[]{:S(2)}, u32[]{:S(2)}) collective-permute-start(f32[8,512]{1,0:T(8,128)S(1)} %reduce_sum.154), channel_id=1, source_target_pairs={{0,12},{2,14},{1,13},{3,15},{16,28},{18,30},{17,29},{19,31}} | collective-permute-start | bytes 49160 | tf_op jit(solution)/shard_map/ppermute | solution.py:31
  124.6 11.2 %collective-permute-start.7 = (f32[8,512]{1,0:T(8,128)S(1)}, f32[8,512]{1,0:T(8,128)S(1)}, u32[]{:S(2)}, u32[]{:S(2)}) collective-permute-start(f32[8,512]{1,0:T(8,128)S(1)} %reduce_sum.154), channel_id=1, source_target_pairs={{0,10},{2,12},{4,14},{1,11},{3,13},{5,15},{16,26},{18,28},{20,30},... | collective-permute-start | bytes 49160 | tf_op jit(solution)/shard_map/ppermute | solution.py:31
  125.9 9.9 %collective-permute-start.6 = (f32[8,512]{1,0:T(8,128)S(1)}, f32[8,512]{1,0:T(8,128)S(1)}, u32[]{:S(2)}, u32[]{:S(2)}) collective-permute-start(f32[8,512]{1,0:T(8,128)S(1)} %reduce_sum.154), channel_id=1, source_target_pairs={{0,8},{2,10},{4,12},{6,14},{1,9},{3,11},{5,13},{7,15},{16,24},{18,... | collective-permute-start | bytes 49160 | tf_op jit(solution)/shard_map/ppermute | solution.py:31
  127.2 8.6 %collective-permute-start.5 = (f32[8,512]{1,0:T(8,128)S(1)}, f32[8,512]{1,0:T(8,128)S(1)}, u32[]{:S(2)}, u32[]{:S(2)}) collective-permute-start(f32[8,512]{1,0:T(8,128)S(1)} %reduce_sum.154), channel_id=1, source_target_pairs={{0,6},{2,8},{4,10},{6,12},{8,14},{1,7},{3,9},{5,11},{7,13},{9,15},... | collective-permute-start | bytes 49160 | tf_op jit(solution)/shard_map/ppermute | solution.py:31
  129.6 6.1 %collective-permute-start.4 = (f32[8,512]{1,0:T(8,128)S(1)}, f32[8,512]{1,0:T(8,128)S(1)}, u32[]{:S(2)}, u32[]{:S(2)}) collective-permute-start(f32[8,512]{1,0:T(8,128)S(1)} %reduce_sum.154), channel_id=1, source_target_pairs={{0,4},{2,6},{4,8},{6,10},{8,12},{10,14},{1,5},{3,7},{5,9},{7,11},{... | collective-permute-start | bytes 49160 | tf_op jit(solution)/shard_map/ppermute | solution.py:31
  131.0 4.8 %collective-permute-start.3 = (f32[8,512]{1,0:T(8,128)S(1)}, f32[8,512]{1,0:T(8,128)S(1)}, u32[]{:S(2)}, u32[]{:S(2)}) collective-permute-start(f32[8,512]{1,0:T(8,128)S(1)} %reduce_sum.154), channel_id=1, source_target_pairs={{0,2},{2,4},{4,6},{6,8},{8,10},{10,12},{12,14},{1,3},{3,5},{5,7},{... | collective-permute-start | bytes 49160 | tf_op jit(solution)/shard_map/ppermute | solution.py:31
where the time goes:
time: 137 us; the launch traced here: 136 us
  local copies, waits for them, and re-layouts  32.7 us (24%)
  blocking collectives  30.7 us (22%)
  matrix products  25 us (18%)
  other arithmetic  23.4 us (17%)
  starting transfers between devices  23 us (17%)
  between operations  1.65 us (1%)
    all_gather x1, blocking collectives, body(): everyone = lax.all_gather(desc[None], 'sec', axis=0, tiled=True)  30.7 us
    ppermute x8, starting transfers between devices, from_behind(): lax.ppermute(value, axis, [(source, source + steps) for source in range(l...  19.3 us
    dot_general x3, matrix products, describe(): jnp.einsum('rtj,bj->rtb', field.reshape(rows, cols // PATCH, PATCH), tabl...  12.5 us
    dot_general x1, matrix products, warp(): out = jnp.einsum('pitw,ptwj->pitj', window, matrix, precision=HIGH)  10.7 us
    add x1, other arithmetic, warp(): vert = vert + weight[:, None, :, None] * part  10.6 us
    reshape x4, local copies, waits for them, and re-layouts, warp(): part = extended[1 + k:1 + k + rows].reshape(prow, PATCH, pcol, PATCH)  10.4 us
    another operation x1, local copies, waits for them, and re-layouts, body(): block = out.reshape(rows // 8, 8, cols // 8, 8).sum(axis=(1, 3))  8.43 us
    reduce_sum x1, other arithmetic, body(): block = out.reshape(rows // 8, 8, cols // 8, 8).sum(axis=(1, 3))  6.95 us
  transfers between devices with their start and end apart: 10, of which 0 were waited for; matrix products, arithmetic and copies ran while one was open for 19% of the time, Pallas kernels for 0%

commit v1 on v0

v1 whole, which is shorter than its diff:
```python
import functools

import jax
import jax.numpy as jnp
import ml_dtypes
import numpy as np
from jax import lax
from jax.experimental import pallas as pl
from jax.experimental.pallas import tpu as pltpu
from jax.sharding import PartitionSpec as P

PATCH = 64
KCOEF = 8
WIN = 8
REG = 4.0
BOX = 8
LANES = 128
PAD = 16
MESH = pl.DeviceIdType.MESH
F32 = jnp.float32
BF16 = jnp.bfloat16


def np_split(value, terms):
    parts = []
    rest = np.asarray(value, np.float64)
    for _ in range(terms):
        part = rest.astype(np.float32).astype(ml_dtypes.bfloat16)
        parts.append(part)
        rest = rest - part.astype(np.float64)
    return parts


def tables(rows):
    index = np.arange(PATCH, dtype=np.float64)
    order = np.arange(KCOEF, dtype=np.float64)
    table = np.sqrt(2.0 / PATCH) * np.cos(np.pi * (index[None, :] + 0.5) * order[:, None] / PATCH)
    table = table * np.where(order == 0, np.sqrt(0.5), 1.0)[:, None]
    table = table.astype(np.float32).astype(np.float64)
    zero = np.zeros((KCOEF, rows), ml_dtypes.bfloat16)
    first = np.concatenate(np_split(table, 3) + [zero], axis=0)
    ext = rows + 2 * PAD
    slope = np.zeros((KCOEF, ext))
    slope[:, PAD + 1 : PAD + 1 + rows] += 0.5 * table
    slope[:, PAD - 1 : PAD - 1 + rows] -= 0.5 * table
    second = np_split(slope, 3) + [np.zeros((KCOEF, ext), ml_dtypes.bfloat16)]
    for k in range(-1, 3):
        sums = np.zeros((rows // BOX, ext))
        for r in range(rows):
            sums[r // BOX, PAD + r + k] = 1.0
        second.append(sums.astype(ml_dtypes.bfloat16))
    second = np.concatenate(second, axis=0)
    column = np.stack([np.tile(part.T, (1, LANES // KCOEF)) for part in np_split(table, 3)])
    return first, second, column


def split(value, terms):
    parts = []
    for _ in range(terms):
        part = value.astype(BF16)
        parts.append(part)
        value = value - part.astype(F32)
    return parts


def dot(a, b):
    return jnp.dot(a, b, preferred_element_type=F32)


def to_groups(value, width):
    count = value.shape[1] // width
    return jnp.concatenate([value[:, g * width : (g + 1) * width] for g in range(count)], axis=0)


def from_groups(value, count):
    rows = value.shape[0] // count
    return jnp.concatenate([value[g * rows : (g + 1) * rows] for g in range(count)], axis=1)


def taps(shift):
    return (
        -shift * (shift - 1.0) * (shift - 2.0) * (1.0 / 6.0),
        (shift + 1.0) * (shift - 1.0) * (shift - 2.0) * 0.5,
        -(shift + 1.0) * shift * (shift - 2.0) * 0.5,
        (shift + 1.0) * shift * (shift - 1.0) * (1.0 / 6.0),
    )


def stacked(value, times):
    return value if times == 1 else jnp.concatenate([value] * times, axis=0)


def kernel(
    n, tiles, kf_ref, off_ref, first_ref, second_ref, column_ref, x_hbm,
    out_hbm, field_ref, pyr_ref,
    xext, coldct, expand, pool, compact, comm, shifted, vert, weights, normal, obuf, brecv, bsend, wsum,
    load_sem, store_sem, halo_ssem, halo_rsem, ssem, rsem, bssem, brsem,
):
    me = lax.axis_index("sec")
    mt = lax.axis_index("tile")
    rows, cols = obuf.shape
    group = LANES // KCOEF * PATCH
    groups = cols // group
    blocks = cols // LANES
    sums = rows // BOX

    load = pltpu.make_async_copy(x_hbm.at[0], xext.at[pl.ds(PAD, rows)], load_sem)
    load.start()

    barrier = pltpu.get_barrier_semaphore()

    def greet(q, carry):
        pl.semaphore_signal(barrier, inc=1, device_id={"sec": q}, device_id_type=MESH)
        return carry

    lax.fori_loop(0, me, greet, 0)

    @pl.when(mt > 0)
    def _():
        pl.semaphore_signal(barrier, inc=1, device_id={"tile": mt - 1}, device_id_type=MESH)

    @pl.when(mt < tiles - 1)
    def _():
        pl.semaphore_signal(barrier, inc=1, device_id={"tile": mt + 1}, device_id_type=MESH)

    lane = lax.broadcasted_iota(jnp.int32, (PATCH, LANES), 1)
    for term in range(3):
        base = column_ref[term].astype(F32)
        for p in range(group // PATCH):
            coldct[term, p * PATCH : (p + 1) * PATCH, :] = jnp.where(
                lane // KCOEF == p, base, 0.0
            ).astype(BF16)

    load.wait()

    def first_dct(g):
        part = dot(first_ref[...], xext[PAD : PAD + rows, g * group : (g + 1) * group])
        return part[0:KCOEF] + part[KCOEF : 2 * KCOEF] + part[2 * KCOEF : 3 * KCOEF]

    t_rows = [first_dct(g) for g in range(groups)]
    t_group = jnp.concatenate(t_rows, axis=0)
    parts = split(t_group, 2)
    size = t_group.shape[0]
    wide = dot(jnp.concatenate(parts, axis=0), coldct[0])
    desc = from_groups(wide[:size] + wide[size:] + dot(parts[0], coldct[1]), groups).astype(BF16)
    comm[me] = desc

    pl.semaphore_wait(
        barrier,
        (n - 1 - me) + (mt > 0).astype(jnp.int32) + (mt < tiles - 1).astype(jnp.int32),
    )

    def desc_copy(target):
        return pltpu.make_async_remote_copy(
            src_ref=comm.at[me], dst_ref=comm.at[me], send_sem=ssem.at[target], recv_sem=rsem.at[me],
            device_id={"sec": target}, device_id_type=MESH,
        )

    def send_desc(step, carry):
        desc_copy(n - 1 - step).start()
        return carry

    lax.fori_loop(0, n - 1 - me, send_desc, 0)

    to_next = pltpu.make_async_remote_copy(
        src_ref=x_hbm.at[0, pl.ds(rows - PAD, PAD)], dst_ref=xext.at[pl.ds(0, PAD)],
        send_sem=halo_ssem.at[0], recv_sem=halo_rsem.at[0],
        device_id={"tile": jnp.minimum(mt + 1, tiles - 1)}, device_id_type=MESH,
    )
    to_last = pltpu.make_async_remote_copy(
        src_ref=x_hbm.at[0, pl.ds(0, PAD)], dst_ref=xext.at[pl.ds(PAD + rows, PAD)],
        send_sem=halo_ssem.at[1], recv_sem=halo_rsem.at[1],
        device_id={"tile": jnp.maximum(mt - 1, 0)}, device_id_type=MESH,
    )

    @pl.when(mt < tiles - 1)
    def _():
        to_next.start()

    @pl.when(mt > 0)
    def _():
        to_last.start()

    @pl.when(mt == 0)
    def _():
        xext[0:PAD, :] = jnp.zeros((PAD, cols), BF16)

    @pl.when(mt == tiles - 1)
    def _():
        xext[PAD + rows : 2 * PAD + rows, :] = jnp.zeros((PAD, cols), BF16)

    row_of = lax.broadcasted_iota(jnp.int32, (LANES, group), 0)
    col_of = lax.broadcasted_iota(jnp.int32, (LANES, group), 1)
    expand[...] = jnp.where(row_of // KCOEF == col_of // PATCH, 1.0, 0.0).astype(BF16)
    row_of = lax.broadcasted_iota(jnp.int32, (group, LANES), 0)
    col_of = lax.broadcasted_iota(jnp.int32, (group, LANES), 1)
    pool[...] = jnp.where(row_of // BOX == col_of, 1.0, 0.0).astype(BF16)
    row_of = lax.broadcasted_iota(jnp.int32, compact.shape, 0)
    col_of = lax.broadcasted_iota(jnp.int32, compact.shape, 1)
    compact[...] = jnp.where(row_of // KCOEF == col_of, 1.0, 0.0).astype(BF16)
    zeros = jnp.zeros((vert.shape[0], LANES), F32)
    vert[:, 0:LANES] = zeros
    vert[:, LANES + cols : 2 * LANES + cols] = zeros

    t_full = jnp.concatenate(t_rows, axis=1)
    where = lax.broadcasted_iota(jnp.int32, (KCOEF, cols), 1)
    after = jnp.where(where == cols - 1, 0.0, pltpu.roll(t_full, cols - 1, 1))
    before = jnp.where(where == 0, 0.0, pltpu.roll(t_full, 1, 1))
    tx_group = to_groups((after - before) * 0.5, group)

    @pl.when(mt < tiles - 1)
    def _():
        to_last.wait_recv()

    @pl.when(mt > 0)
    def _():
        to_next.wait_recv()

    ty_rows = []
    for g in range(groups):
        part = dot(second_ref[...], xext[:, g * group : (g + 1) * group])
        ty_rows.append(part[0:KCOEF] + part[KCOEF : 2 * KCOEF] + part[2 * KCOEF : 3 * KCOEF])
        for k in range(4):
            at = 4 * KCOEF + k * sums
            shifted[k, 0:sums, g * group : (g + 1) * group] = part[at : at + sums]
    ty_group = jnp.concatenate(ty_rows, axis=0)

    both = jnp.concatenate([tx_group, ty_group], axis=0)
    parts = split(both, 3)
    size = both.shape[0]
    wide = dot(jnp.concatenate(parts, axis=0), coldct[0])
    mid = dot(jnp.concatenate(parts[:2], axis=0), coldct[1])
    slopes = wide[:size] + (wide[size : 2 * size] + mid[:size]) + (
        wide[2 * size :] + mid[size:] + dot(parts[0], coldct[2])
    )
    half = size // 2
    dx = from_groups(slopes[:half], groups)
    dy = from_groups(slopes[half:], groups)

    def row_total(value):
        for step in (4, 2, 1):
            value = value + pltpu.roll(value, step, 0)
        return value

    def spread(values):
        lhs = jnp.concatenate([to_groups(v, LANES) for v in values], axis=0)
        size = lhs.shape[0]
        wide = dot(jnp.concatenate(split(lhs, 3), axis=0), expand[...])
        total = wide[:size] + (wide[size : 2 * size] + wide[2 * size :])
        step = size // len(values)
        return [from_groups(total[i * step : (i + 1) * step], groups) for i in range(len(values))]

    def narrow(values):
        lhs = jnp.concatenate(values, axis=0)
        size = lhs.shape[0]
        wide = dot(jnp.concatenate(split(lhs, 3), axis=0), compact[...])
        total = wide[:size] + (wide[size : 2 * size] + wide[2 * size :])
        step = size // len(values)
        return [total[i * step : (i + 1) * step] for i in range(len(values))]

    normals = [row_total(dx * dx), row_total(dx * dy), row_total(dy * dy)]
    gxx, gxy, gyy = spread(normals)
    gxx = gxx + REG
    gyy = gyy + REG
    normal[0] = gxx
    normal[1] = gxy
    normal[2] = gyy
    normal[3] = 1.0 / (gxx * gyy - gxy * gxy)

    def prepare(v, carry):
        at = pl.ds(pl.multiple_of(v * LANES, LANES), LANES)
        block = xext[:, at].astype(F32)
        height = block.shape[0]
        for k in range(4):
            moved = block if k == 1 else pltpu.roll(block, (height - (k - 1)) % height, 0)
            shifted[k, sums : sums + rows, at] = moved[PAD : PAD + rows]
        return carry

    lax.fori_loop(0, blocks, prepare, 0)

    def wait_desc(q, carry):
        pltpu.make_async_remote_copy(
            src_ref=comm.at[q], dst_ref=comm.at[q], send_sem=ssem.at[q], recv_sem=rsem.at[q],
            device_id={"sec": q}, device_id_type=MESH,
        ).wait_recv()
        return carry

    lax.fori_loop(0, me, wait_desc, 0)

    keyref = comm[kf_ref[0]].astype(F32)
    predref = jnp.where(me > 0, comm[jnp.maximum(me - 1, 0)].astype(F32), 0.0)
    diff = 0.5 * (keyref + predref) - desc.astype(F32)
    slants = [row_total(dx * diff), row_total(dy * diff)]
    bx, by = spread(slants)
    ux = (normal[2] * bx - normal[1] * by) * normal[3]
    uy = (normal[0] * by - normal[1] * bx) * normal[3]
    for k, weight in enumerate(taps(ux)):
        weights[k] = weight
    for k, weight in enumerate(taps(uy)):
        weights[4 + k] = weight

    lane8 = lax.broadcasted_iota(jnp.int32, (BOX, LANES), 1)

    def vertical(low, count):
        times = count // BOX

        def run(v, carry):
            at = pl.ds(pl.multiple_of(v * LANES, LANES), LANES)
            total = stacked(weights[4, :, at], times) * shifted[0, low : low + count, at]
            for k in range(1, 4):
                total = total + stacked(weights[4 + k, :, at], times) * shifted[k, low : low + count, at]
            vert[low : low + count, pl.ds(pl.multiple_of((v + 1) * LANES, LANES), LANES)] = total
            return carry

        return run

    def horizontal(low, count, store):
        times = count // BOX

        def run(v, carry):
            span = slice(low, low + count)
            left = vert[span, pl.ds(pl.multiple_of(v * LANES, LANES), LANES)]
            center = vert[span, pl.ds(pl.multiple_of((v + 1) * LANES, LANES), LANES)]
            right = vert[span, pl.ds(pl.multiple_of((v + 2) * LANES, LANES), LANES)]
            lanes = stacked(lane8, times)
            even = jnp.where(lanes >= 96, left, center)
            odd = jnp.where(lanes < 32, right, center)
            even = pltpu.roll(even, (LANES - off_ref[0, 2 * v]) % LANES, 1)
            odd = pltpu.roll(odd, (LANES - off_ref[0, 2 * v + 1]) % LANES, 1)
            at = pl.ds(pl.multiple_of(v * LANES, LANES), LANES)
            total = None
            for k in range(-1, 3):
                mine = ((lanes - k + LANES) % LANES) < PATCH
                both = jnp.where(mine, even, odd)
                if k != 0:
                    both = pltpu.roll(both, (LANES - k) % LANES, 1)
                term = stacked(weights[k + 1, :, at], times) * both
                total = term if total is None else total + term
            store(at, total)
            return carry

        return run

    def store_sums(at, value):
        wsum[:, at] = value

    def store_rows(at, value):
        obuf[:, at] = value.astype(BF16)

    lax.fori_loop(0, blocks, vertical(0, sums), 0, unroll=4)
    lax.fori_loop(0, blocks, horizontal(0, sums, store_sums), 0, unroll=4)
    lhs = to_groups(wsum[...], group)
    size = lhs.shape[0]
    wide = dot(jnp.concatenate(split(lhs, 3), axis=0), pool[...])
    block = from_groups(wide[:size] + (wide[size : 2 * size] + wide[2 * size :]), groups)
    bsend[...] = block

    def block_copy(d):
        return pltpu.make_async_remote_copy(
            src_ref=bsend, dst_ref=brecv.at[d - 1], send_sem=bssem.at[d - 1], recv_sem=brsem.at[d - 1],
            device_id={"sec": jnp.minimum(me + d, n - 1)}, device_id_type=MESH,
        )

    reach = min(WIN, n)
    for d in range(reach - 1, 0, -1):
        @pl.when(me + d < n)
        def _():
            block_copy(d).start()

    lax.fori_loop(0, blocks, vertical(sums, rows), 0)
    lax.fori_loop(0, blocks, horizontal(sums, rows, store_rows), 0)
    store = pltpu.make_async_copy(obuf, out_hbm.at[0], store_sem)
    store.start()

    gxx, gxy, gyy, bx, by = narrow(normals + slants)
    gxx = gxx + REG
    gyy = gyy + REG
    det = gxx * gyy - gxy * gxy
    ux = (gyy * bx - gxy * by) / det
    uy = (gxx * by - gxy * bx) / det
    field_ref[0, 0] = ux[0:1]
    field_ref[0, 1] = uy[0:1]

    pyr_ref[0] = block
    for d in range(1, reach):
        @pl.when(me >= d)
        def _():
            block_copy(d).wait_recv()
            pyr_ref[0] = pyr_ref[0] + brecv[d - 1]
    pyr_ref[0] = pyr_ref[0] * (1.0 / (BOX * BOX * WIN))

    def sent_desc(step, carry):
        desc_copy(n - 1 - step).wait_send()
        return carry

    lax.fori_loop(0, n - 1 - me, sent_desc, 0)
    for d in range(reach - 1, 0, -1):
        @pl.when(me + d < n)
        def _():
            block_copy(d).wait_send()

    @pl.when(mt < tiles - 1)
    def _():
        to_next.wait_send()

    @pl.when(mt > 0)
    def _():
        to_last.wait_send()

    store.wait()


def body(n, tiles, image, keyframe, offsets):
    _, rows, cols = image.shape
    first, second, column = tables(rows)
    ext = rows + 2 * PAD
    sums = rows // BOX
    coefs = cols // PATCH * KCOEF
    group = LANES // KCOEF * PATCH
    smem = pl.BlockSpec(memory_space=pltpu.SMEM)
    vmem = pl.BlockSpec(memory_space=pltpu.VMEM)
    hbm = pl.BlockSpec(memory_space=pl.ANY)
    dma = pltpu.SemaphoreType.DMA
    return pl.pallas_call(
        functools.partial(kernel, n, tiles),
        out_shape=(
            jax.ShapeDtypeStruct(image.shape, BF16),
            jax.ShapeDtypeStruct((1, 2, 1, cols // PATCH), F32),
            jax.ShapeDtypeStruct((1, sums, cols // BOX), F32),
        ),
        in_specs=[smem, smem, vmem, vmem, vmem, hbm],
        out_specs=(hbm, vmem, vmem),
        scratch_shapes=[
            pltpu.VMEM((ext, cols), BF16),
            pltpu.VMEM((3, group, LANES), BF16),
            pltpu.VMEM((LANES, group), BF16),
            pltpu.VMEM((group, LANES), BF16),
            pltpu.VMEM((coefs, cols // PATCH), BF16),
            pltpu.VMEM((n, KCOEF, coefs), BF16),
            pltpu.VMEM((4, sums + rows, cols), F32),
            pltpu.VMEM((sums + rows, cols + 2 * LANES), F32),
            pltpu.VMEM((8, KCOEF, cols), F32),
            pltpu.VMEM((4, KCOEF, cols), F32),
            pltpu.VMEM((rows, cols), BF16),
            pltpu.VMEM((WIN - 1, sums, cols // BOX), F32),
            pltpu.VMEM((sums, cols // BOX), F32),
            pltpu.VMEM((sums, cols), F32),
            dma,
            dma,
            dma((2,)),
            dma((2,)),
            dma((n,)),
            dma((n,)),
            dma((WIN - 1,)),
            dma((WIN - 1,)),
        ],
        compiler_params=pltpu.CompilerParams(collective_id=0, has_side_effects=True),
    )(keyframe, offsets, jnp.asarray(first), jnp.asarray(second), jnp.asarray(column), image)


def solution(mesh):
    return jax.shard_map(
        functools.partial(body, mesh.shape["sec"], mesh.shape["tile"]),
        mesh=mesh,
        in_specs=(P(("slab", "sec"), "tile", None), P(("slab", "sec")), P(("slab", "sec"), None)),
        out_specs=(
            P(("slab", "sec"), "tile", None),
            P(("slab", "sec"), None, "tile", None),
            P(("slab", "sec"), "tile", None),
        ),
        check_vma=False,
    )
```

time: 137 us -> 24.4 us (0.18)
  the two profiles are of different devices: /device:TPU:0 before, /device:TPU:1 now
where the time goes in v1:
time: 24.4 us; the launch traced here: 24.2 us
  Pallas kernels  19.8 us (81%)
  local copies, waits for them, and re-layouts  3.05 us (12%)
  between operations  1.3 us (5%)
    pallas_call x1, Pallas kernels, body(): pl.pallas_call(functools.partial(kernel, n, tiles), out_shape=(jax.ShapeD...  19.8 us
    unnamed x7, local copies, waits for them, and re-layouts  3.05 us

profile of v1, /device:TPU:1, one launch (start us, length us, event | category | flops | bytes accessed | tf_op | source)
XLA Modules:
  0.0 24.2 jit_solution(6886858753523410613)
XLA Ops:
  1.3 19.8 %shard_map.85 = (bf16[1,64,4096]{2,1,0:T(8,128)(2,1)}, f32[1,2,1,64]{3,2,1,0:T(1,128)}, f32[1,8,512]{2,1,0:T(8,128)}) custom-call(s32[1]{0:T(128)S(6)} %copy.12.kf_ref, s32[1,64]{1,0:T(1,128)} %off_ref.1, bf16[32,64]{1,0:T(8,128)(2,1)} %constant.6.clone.first_ref, bf16[64,96]{1,0:T(8,128)(2,1)} %constant.7.clone.second_ref, ...), custom_call_target="tpu_custom_call" | custom-call | tf_op jit(solution)/shard_map/pallas_call | solution.py:424
  21.1 0.0 copy-start.1
  21.1 0.0 copy-start
  21.1 1.9 %copy.13 = bf16[1,64,4096]{2,1,0:T(8,128)(2,1)} copy(bf16[1,64,4096]{2,1,0:T(8,128)(2,1)} %get-tuple-element.6) | data formatting | bytes 1048576
  23.0 0.0 copy-done.1
  23.0 0.6 %copy.14 = f32[1,2,1,64]{3,2,1,0:T(1,128)} copy(f32[1,2,1,64]{3,2,1,0:T(1,128)S(1)} %copy-done.1) | data formatting | bytes 1024
  23.6 0.0 copy-done
  23.6 0.6 %copy.15 = f32[1,8,512]{2,1,0:T(8,128)} copy(f32[1,8,512]{2,1,0:T(8,128)S(1)} %copy-done) | data formatting | bytes 32768
Async XLA Ops:
  21.1 1.9 %copy-start.1 = (f32[1,2,1,64]{3,2,1,0:T(1,128)S(1)}, f32[1,2,1,64]{3,2,1,0:T(1,128)}, u32[]{:S(2)}) copy-start(f32[1,2,1,64]{3,2,1,0:T(1,128)} %get-tuple-element.7) | copy-start | bytes 1540
  21.1 2.5 %copy-start = (f32[1,8,512]{2,1,0:T(8,128)S(1)}, f32[1,8,512]{2,1,0:T(8,128)}, u32[]{:S(2)}) copy-start(f32[1,8,512]{2,1,0:T(8,128)} %get-tuple-element.8) | copy-start | bytes 49156

commit v2 on v1

--- a/solution.py
+++ b/solution.py
@@ -91,23 +91,33 @@
 
 
 def kernel(
-    n, tiles, kf_ref, off_ref, first_ref, second_ref, column_ref, x_hbm,
-    out_hbm, field_ref, pyr_ref,
-    xext, coldct, expand, pool, compact, comm, shifted, vert, weights, normal, obuf, brecv, bsend, wsum,
-    load_sem, store_sem, halo_ssem, halo_rsem, ssem, rsem, bssem, brsem,
+    n, tiles, kf_hbm, off_hbm, first_hbm, second_hbm, column_hbm, x_hbm,
+    obuf, field_ref, pyr_ref,
+    kf_ref, off_ref, first_ref, second_ref, column_ref, xext, coldct, expand, pool, compact, comm, shifted, vert, weights, normal, brecv, bsend, wsum,
+    load_sem, table_sem, halo_ssem, halo_rsem, ssem, rsem, bssem, brsem,
 ):
     me = lax.axis_index("sec")
     mt = lax.axis_index("tile")
-    rows, cols = obuf.shape
+    _, rows, cols = obuf.shape
     group = LANES // KCOEF * PATCH
     groups = cols // group
     blocks = cols // LANES
     sums = rows // BOX
 
+    barrier = pltpu.get_barrier_semaphore()
     load = pltpu.make_async_copy(x_hbm.at[0], xext.at[pl.ds(PAD, rows)], load_sem)
+    fetches = [
+        pltpu.make_async_copy(source, target, table_sem.at[i])
+        for i, (source, target) in enumerate((
+            (column_hbm, column_ref), (first_hbm, first_ref), (second_hbm, second_ref),
+            (kf_hbm, kf_ref), (off_hbm, off_ref),
+        ))
+    ]
+    fetches[0].start()
+    fetches[1].start()
     load.start()
-
-    barrier = pltpu.get_barrier_semaphore()
+    for fetch in fetches[2:]:
+        fetch.start()
 
     def greet(q, carry):
         pl.semaphore_signal(barrier, inc=1, device_id={"sec": q}, device_id_type=MESH)
@@ -123,6 +133,7 @@
     def _():
         pl.semaphore_signal(barrier, inc=1, device_id={"tile": mt + 1}, device_id_type=MESH)
 
+    fetches[0].wait()
     lane = lax.broadcasted_iota(jnp.int32, (PATCH, LANES), 1)
     for term in range(3):
         base = column_ref[term].astype(F32)
@@ -131,6 +142,7 @@
                 lane // KCOEF == p, base, 0.0
             ).astype(BF16)
 
+    fetches[1].wait()
     load.wait()
 
     def first_dct(g):
@@ -216,6 +228,7 @@
     def _():
         to_next.wait_recv()
 
+    fetches[2].wait()
     ty_rows = []
     for g in range(groups):
         part = dot(second_ref[...], xext[:, g * group : (g + 1) * group])
@@ -276,7 +289,12 @@
             shifted[k, sums : sums + rows, at] = moved[PAD : PAD + rows]
         return carry
 
-    lax.fori_loop(0, blocks, prepare, 0)
+    @pl.when(me >= n // 2)
+    def _():
+        lax.fori_loop(0, blocks, prepare, 0, unroll=4)
+
+    fetches[3].wait()
+    fetches[4].wait()
 
     def wait_desc(q, carry):
         pltpu.make_async_remote_copy(
@@ -345,10 +363,10 @@
         wsum[:, at] = value
 
     def store_rows(at, value):
-        obuf[:, at] = value.astype(BF16)
-
-    lax.fori_loop(0, blocks, vertical(0, sums), 0, unroll=4)
-    lax.fori_loop(0, blocks, horizontal(0, sums, store_sums), 0, unroll=4)
+        obuf[0, :, at] = value.astype(BF16)
+
+    lax.fori_loop(0, blocks, vertical(0, sums), 0, unroll=16)
+    lax.fori_loop(0, blocks, horizontal(0, sums, store_sums), 0, unroll=16)
     lhs = to_groups(wsum[...], group)
     size = lhs.shape[0]
     wide = dot(jnp.concatenate(split(lhs, 3), axis=0), pool[...])
@@ -367,10 +385,12 @@
         def _():
             block_copy(d).start()
 
-    lax.fori_loop(0, blocks, vertical(sums, rows), 0)
-    lax.fori_loop(0, blocks, horizontal(sums, rows, store_rows), 0)
-    store = pltpu.make_async_copy(obuf, out_hbm.at[0], store_sem)
-    store.start()
+    @pl.when(me < n // 2)
+    def _():
+        lax.fori_loop(0, blocks, prepare, 0, unroll=4)
+
+    lax.fori_loop(0, blocks, vertical(sums, rows), 0, unroll=2)
+    lax.fori_loop(0, blocks, horizontal(sums, rows, store_rows), 0, unroll=4)
 
     gxx, gxy, gyy, bx, by = narrow(normals + slants)
     gxx = gxx + REG
@@ -407,8 +427,6 @@
     def _():
         to_last.wait_send()
 
-    store.wait()
-
 
 def body(n, tiles, image, keyframe, offsets):
     _, rows, cols = image.shape
@@ -417,20 +435,24 @@
     sums = rows // BOX
     coefs = cols // PATCH * KCOEF
     group = LANES // KCOEF * PATCH
-    smem = pl.BlockSpec(memory_space=pltpu.SMEM)
     vmem = pl.BlockSpec(memory_space=pltpu.VMEM)
-    hbm = pl.BlockSpec(memory_space=pl.ANY)
+    hbm = pl.BlockSpec(memory_space=pltpu.HBM)
     dma = pltpu.SemaphoreType.DMA
     return pl.pallas_call(
         functools.partial(kernel, n, tiles),
         out_shape=(
-            jax.ShapeDtypeStruct(image.shape, BF16),
-            jax.ShapeDtypeStruct((1, 2, 1, cols // PATCH), F32),
-            jax.ShapeDtypeStruct((1, sums, cols // BOX), F32),
+            pltpu.VMEM(image.shape, BF16),
+            pltpu.VMEM((1, 2, 1, cols // PATCH), F32),
+            pltpu.VMEM((1, sums, cols // BOX), F32),
         ),
-        in_specs=[smem, smem, vmem, vmem, vmem, hbm],
-        out_specs=(hbm, vmem, vmem),
+        in_specs=[hbm] * 6,
+        out_specs=(vmem, vmem, vmem),
         scratch_shapes=[
+            pltpu.SMEM((1,), jnp.int32),
+            pltpu.SMEM((1, cols // PATCH), jnp.int32),
+            pltpu.VMEM(first.shape, BF16),
+            pltpu.VMEM(second.shape, BF16),
+            pltpu.VMEM(column.shape, BF16),
             pltpu.VMEM((ext, cols), BF16),
             pltpu.VMEM((3, group, LANES), BF16),
             pltpu.VMEM((LANES, group), BF16),
@@ -441,12 +463,11 @@
             pltpu.VMEM((sums + rows, cols + 2 * LANES), F32),
             pltpu.VMEM((8, KCOEF, cols), F32),
             pltpu.VMEM((4, KCOEF, cols), F32),
-            pltpu.VMEM((rows, cols), BF16),
             pltpu.VMEM((WIN - 1, sums, cols // BOX), F32),
             pltpu.VMEM((sums, cols // BOX), F32),
             pltpu.VMEM((sums, cols), F32),
             dma,
-            dma,
+            dma((5,)),
             dma((2,)),
             dma((2,)),
             dma((n,)),

time: 24.4 us -> 17.5 us (0.72)
  Pallas kernels: 19.8 us -> 14.1 us
  local copies, waits for them, and re-layouts: 3.05 us -> 1.96 us
    pallas_call x1, Pallas kernels: 19.8 us -> 14.1 us  [body(): pl.pallas_call(functools.partial(kernel, n, tiles), out_shape=(pltpu.VMEM...]
    unnamed x7 -> x3, local copies, waits for them, and re-layouts: 3.05 us -> 1.96 us
where the time goes in v2:
time: 17.5 us; the launch traced here: 17.4 us
  Pallas kernels  14.1 us (81%)
  local copies, waits for them, and re-layouts  1.96 us (11%)
  between operations  1.29 us (7%)
    pallas_call x1, Pallas kernels, body(): pl.pallas_call(functools.partial(kernel, n, tiles), out_shape=(pltpu.VMEM...  14.1 us
    unnamed x3, local copies, waits for them, and re-layouts  1.96 us

profile of v2, /device:TPU:1, one launch (start us, length us, event | category | flops | bytes accessed | tf_op | source)
XLA Modules:
  0.0 17.4 jit_solution(17886069322463274393)
XLA Ops:
  1.3 14.1 %shard_map.85 = (bf16[1,64,4096]{2,1,0:T(8,128)(2,1)S(1)}, f32[1,2,1,64]{3,2,1,0:T(1,128)S(1)}, f32[1,8,512]{2,1,0:T(8,128)S(1)}) custom-call(s32[1]{0:T(128)S(6)} %copy.15.kf_hbm, s32[1,64]{1,0:T(1,128)} %off_hbm.1, bf16[32,64]{1,0:T(8,128)(2,1)} %constant.6.clone.first_hbm, bf16[64,96]{1,0:T(8,128)(2,1)} %constant.7.clone.second_hbm, ...), custom_call_target="tpu_custom_call" | custom-call | tf_op jit(solution)/shard_map/pallas_call | solution.py:441
  15.4 0.8 %copy.12 = bf16[1,64,4096]{2,1,0:T(8,128)(2,1)} copy(bf16[1,64,4096]{2,1,0:T(8,128)(2,1)S(1)} %get-tuple-element.3) | data formatting | bytes 1048576
  16.2 0.6 %copy.13 = f32[1,2,1,64]{3,2,1,0:T(1,128)} copy(f32[1,2,1,64]{3,2,1,0:T(1,128)S(1)} %get-tuple-element.4) | data formatting | bytes 1024
  16.8 0.6 %copy.14 = f32[1,8,512]{2,1,0:T(8,128)} copy(f32[1,8,512]{2,1,0:T(8,128)S(1)} %get-tuple-element.5) | data formatting | bytes 32768

commit v3 on v2

--- a/solution.py
+++ b/solution.py
@@ -86,14 +86,10 @@
     )
 
 
-def stacked(value, times):
-    return value if times == 1 else jnp.concatenate([value] * times, axis=0)
-
-
 def kernel(
     n, tiles, kf_hbm, off_hbm, first_hbm, second_hbm, column_hbm, x_hbm,
     obuf, field_ref, pyr_ref,
-    kf_ref, off_ref, first_ref, second_ref, column_ref, xext, coldct, expand, pool, compact, comm, shifted, vert, weights, normal, brecv, bsend, wsum,
+    kf_ref, off_ref, first_ref, second_ref, column_ref, xext, coldct, expand, pool, compact, comm, shifted, weights, normal, brecv, bsend, wsum,
     load_sem, table_sem, halo_ssem, halo_rsem, ssem, rsem, bssem, brsem,
 ):
     me = lax.axis_index("sec")
@@ -105,7 +101,14 @@
     sums = rows // BOX
 
     barrier = pltpu.get_barrier_semaphore()
-    load = pltpu.make_async_copy(x_hbm.at[0], xext.at[pl.ds(PAD, rows)], load_sem)
+    loads = [
+        pltpu.make_async_copy(
+            x_hbm.at[0, :, pl.ds(g * group, group)],
+            xext.at[pl.ds(PAD, rows), pl.ds(g * group, group)],
+            load_sem.at[g],
+        )
+        for g in range(groups)
+    ]
     fetches = [
         pltpu.make_async_copy(source, target, table_sem.at[i])
         for i, (source, target) in enumerate((
@@ -115,7 +118,8 @@
     ]
     fetches[0].start()
     fetches[1].start()
-    load.start()
+    for load in loads:
+        load.start()
     for fetch in fetches[2:]:
         fetch.start()
 
@@ -142,10 +146,19 @@
                 lane // KCOEF == p, base, 0.0
             ).astype(BF16)
 
+    row_of = lax.broadcasted_iota(jnp.int32, (LANES, group), 0)
+    col_of = lax.broadcasted_iota(jnp.int32, (LANES, group), 1)
+    expand[...] = jnp.where(row_of // KCOEF == col_of // PATCH, 1.0, 0.0).astype(BF16)
+    row_of = lax.broadcasted_iota(jnp.int32, (group, LANES), 0)
+    col_of = lax.broadcasted_iota(jnp.int32, (group, LANES), 1)
+    pool[...] = jnp.where(row_of // BOX == col_of, 1.0, 0.0).astype(BF16)
+    row_of = lax.broadcasted_iota(jnp.int32, compact.shape, 0)
+    col_of = lax.broadcasted_iota(jnp.int32, compact.shape, 1)
+    compact[...] = jnp.where(row_of // KCOEF == col_of, 1.0, 0.0).astype(BF16)
     fetches[1].wait()
-    load.wait()
 
     def first_dct(g):
+        loads[g].wait()
         part = dot(first_ref[...], xext[PAD : PAD + rows, g * group : (g + 1) * group])
         return part[0:KCOEF] + part[KCOEF : 2 * KCOEF] + part[2 * KCOEF : 3 * KCOEF]
 
@@ -201,24 +214,23 @@
     def _():
         xext[PAD + rows : 2 * PAD + rows, :] = jnp.zeros((PAD, cols), BF16)
 
-    row_of = lax.broadcasted_iota(jnp.int32, (LANES, group), 0)
-    col_of = lax.broadcasted_iota(jnp.int32, (LANES, group), 1)
-    expand[...] = jnp.where(row_of // KCOEF == col_of // PATCH, 1.0, 0.0).astype(BF16)
-    row_of = lax.broadcasted_iota(jnp.int32, (group, LANES), 0)
-    col_of = lax.broadcasted_iota(jnp.int32, (group, LANES), 1)
-    pool[...] = jnp.where(row_of // BOX == col_of, 1.0, 0.0).astype(BF16)
-    row_of = lax.broadcasted_iota(jnp.int32, compact.shape, 0)
-    col_of = lax.broadcasted_iota(jnp.int32, compact.shape, 1)
-    compact[...] = jnp.where(row_of // KCOEF == col_of, 1.0, 0.0).astype(BF16)
-    zeros = jnp.zeros((vert.shape[0], LANES), F32)
-    vert[:, 0:LANES] = zeros
-    vert[:, LANES + cols : 2 * LANES + cols] = zeros
-
     t_full = jnp.concatenate(t_rows, axis=1)
     where = lax.broadcasted_iota(jnp.int32, (KCOEF, cols), 1)
     after = jnp.where(where == cols - 1, 0.0, pltpu.roll(t_full, cols - 1, 1))
     before = jnp.where(where == 0, 0.0, pltpu.roll(t_full, 1, 1))
     tx_group = to_groups((after - before) * 0.5, group)
+
+    def slope_of(value):
+        parts = split(value, 3)
+        size = value.shape[0]
+        wide = dot(jnp.concatenate(parts, axis=0), coldct[0])
+        mid = dot(jnp.concatenate(parts[:2], axis=0), coldct[1])
+        total = wide[:size] + (wide[size : 2 * size] + mid[:size]) + (
+            wide[2 * size :] + mid[size:] + dot(parts[0], coldct[2])
+        )
+        return from_groups(total, groups)
+
+    dx = slope_of(tx_group)
 
     @pl.when(mt < tiles - 1)
     def _():
@@ -238,17 +250,7 @@
             shifted[k, 0:sums, g * group : (g + 1) * group] = part[at : at + sums]
     ty_group = jnp.concatenate(ty_rows, axis=0)
 
-    both = jnp.concatenate([tx_group, ty_group], axis=0)
-    parts = split(both, 3)
-    size = both.shape[0]
-    wide = dot(jnp.concatenate(parts, axis=0), coldct[0])
-    mid = dot(jnp.concatenate(parts[:2], axis=0), coldct[1])
-    slopes = wide[:size] + (wide[size : 2 * size] + mid[:size]) + (
-        wide[2 * size :] + mid[size:] + dot(parts[0], coldct[2])
-    )
-    half = size // 2
-    dx = from_groups(slopes[:half], groups)
-    dy = from_groups(slopes[half:], groups)
+    dy = slope_of(ty_group)
 
     def row_total(value):
         for step in (4, 2, 1):
@@ -318,55 +320,53 @@
         weights[4 + k] = weight
 
     lane8 = lax.broadcasted_iota(jnp.int32, (BOX, LANES), 1)
-
-    def vertical(low, count):
-        times = count // BOX
-
-        def run(v, carry):
-            at = pl.ds(pl.multiple_of(v * LANES, LANES), LANES)
-            total = stacked(weights[4, :, at], times) * shifted[0, low : low + count, at]
+    takes = [((lane8 - k) & (LANES - 1)) < PATCH for k in range(-1, 3)]
+    from_left = lane8 >= 96
+    from_right = lane8 < 32
+
+    def vertical(v, low, count):
+        at = slice(v * LANES, (v + 1) * LANES)
+        gains = [weights[4 + k, :, at] for k in range(4)]
+        strips = []
+        for r in range(low, low + count, BOX):
+            total = gains[0] * shifted[0, r : r + BOX, at]
             for k in range(1, 4):
-                total = total + stacked(weights[4 + k, :, at], times) * shifted[k, low : low + count, at]
-            vert[low : low + count, pl.ds(pl.multiple_of((v + 1) * LANES, LANES), LANES)] = total
-            return carry
-
-        return run
-
-    def horizontal(low, count, store):
-        times = count // BOX
-
-        def run(v, carry):
-            span = slice(low, low + count)
-            left = vert[span, pl.ds(pl.multiple_of(v * LANES, LANES), LANES)]
-            center = vert[span, pl.ds(pl.multiple_of((v + 1) * LANES, LANES), LANES)]
-            right = vert[span, pl.ds(pl.multiple_of((v + 2) * LANES, LANES), LANES)]
-            lanes = stacked(lane8, times)
-            even = jnp.where(lanes >= 96, left, center)
-            odd = jnp.where(lanes < 32, right, center)
-            even = pltpu.roll(even, (LANES - off_ref[0, 2 * v]) % LANES, 1)
-            odd = pltpu.roll(odd, (LANES - off_ref[0, 2 * v + 1]) % LANES, 1)
-            at = pl.ds(pl.multiple_of(v * LANES, LANES), LANES)
+                total = total + gains[k] * shifted[k, r : r + BOX, at]
+            strips.append(total)
+        return strips
+
+    def horizontal(v, left, center, right, store):
+        at = slice(v * LANES, (v + 1) * LANES)
+        turn_even = (LANES - off_ref[0, 2 * v]) & (LANES - 1)
+        turn_odd = (LANES - off_ref[0, 2 * v + 1]) & (LANES - 1)
+        gains = [weights[k, :, at] for k in range(4)]
+        for r in range(len(center)):
+            even = pltpu.roll(jnp.where(from_left, left[r], center[r]), turn_even, 1)
+            odd = pltpu.roll(jnp.where(from_right, right[r], center[r]), turn_odd, 1)
             total = None
             for k in range(-1, 3):
-                mine = ((lanes - k + LANES) % LANES) < PATCH
-                both = jnp.where(mine, even, odd)
+                both = jnp.where(takes[k + 1], even, odd)
                 if k != 0:
                     both = pltpu.roll(both, (LANES - k) % LANES, 1)
-                term = stacked(weights[k + 1, :, at], times) * both
+                term = gains[k + 1] * both
                 total = term if total is None else total + term
-            store(at, total)
-            return carry
-
-        return run
-
-    def store_sums(at, value):
-        wsum[:, at] = value
-
-    def store_rows(at, value):
-        obuf[0, :, at] = value.astype(BF16)
-
-    lax.fori_loop(0, blocks, vertical(0, sums), 0, unroll=16)
-    lax.fori_loop(0, blocks, horizontal(0, sums, store_sums), 0, unroll=16)
+            store(r * BOX, at, total)
+
+    def warp(low, count, store):
+        blank = [jnp.zeros((BOX, LANES), F32)] * (count // BOX)
+        left, center = blank, vertical(0, low, count)
+        for v in range(blocks):
+            right = vertical(v + 1, low, count) if v + 1 < blocks else blank
+            horizontal(v, left, center, right, store)
+            left, center = center, right
+
+    def store_sums(r, at, value):
+        wsum[r : r + BOX, at] = value
+
+    def store_rows(r, at, value):
+        obuf[0, r : r + BOX, at] = value.astype(BF16)
+
+    warp(0, sums, store_sums)
     lhs = to_groups(wsum[...], group)
     size = lhs.shape[0]
     wide = dot(jnp.concatenate(split(lhs, 3), axis=0), pool[...])
@@ -389,8 +389,7 @@
     def _():
         lax.fori_loop(0, blocks, prepare, 0, unroll=4)
 
-    lax.fori_loop(0, blocks, vertical(sums, rows), 0, unroll=2)
-    lax.fori_loop(0, blocks, horizontal(sums, rows, store_rows), 0, unroll=4)
+    warp(sums, rows, store_rows)
 
     gxx, gxy, gyy, bx, by = narrow(normals + slants)
     gxx = gxx + REG
@@ -426,6 +425,17 @@
     @pl.when(mt > 0)
     def _():
         to_last.wait_send()
+
+
+def write_out(a, b, c, a_out, b_out, c_out, sem):
+    copies = [
+        pltpu.make_async_copy(source, target, sem.at[i])
+        for i, (source, target) in enumerate(((a, a_out), (b, b_out), (c, c_out)))
+    ]
+    for copy in copies:
+        copy.start()
+    for copy in copies:
+        copy.wait()
 
 
 def body(n, tiles, image, keyframe, offsets):
@@ -438,7 +448,7 @@
     vmem = pl.BlockSpec(memory_space=pltpu.VMEM)
     hbm = pl.BlockSpec(memory_space=pltpu.HBM)
     dma = pltpu.SemaphoreType.DMA
-    return pl.pallas_call(
+    results = pl.pallas_call(
         functools.partial(kernel, n, tiles),
         out_shape=(
             pltpu.VMEM(image.shape, BF16),
@@ -460,13 +470,12 @@
             pltpu.VMEM((coefs, cols // PATCH), BF16),
             pltpu.VMEM((n, KCOEF, coefs), BF16),
             pltpu.VMEM((4, sums + rows, cols), F32),
-            pltpu.VMEM((sums + rows, cols + 2 * LANES), F32),
             pltpu.VMEM((8, KCOEF, cols), F32),
             pltpu.VMEM((4, KCOEF, cols), F32),
             pltpu.VMEM((WIN - 1, sums, cols // BOX), F32),
             pltpu.VMEM((sums, cols // BOX), F32),
             pltpu.VMEM((sums, cols), F32),
-            dma,
+            dma((cols // group,)),
             dma((5,)),
             dma((2,)),
             dma((2,)),
@@ -477,6 +486,13 @@
         ],
         compiler_params=pltpu.CompilerParams(collective_id=0, has_side_effects=True),
     )(keyframe, offsets, jnp.asarray(first), jnp.asarray(second), jnp.asarray(column), image)
+    return pl.pallas_call(
+        write_out,
+        out_shape=tuple(jax.ShapeDtypeStruct(r.shape, r.dtype) for r in results),
+        in_specs=[vmem] * 3,
+        out_specs=(hbm,) * 3,
+        scratch_shapes=[dma((3,))],
+    )(*[pltpu.with_memory_space_constraint(r, pltpu.VMEM) for r in results])
 
 
 def solution(mesh):

time: 17.5 us -> 29 us (1.66)
  Pallas kernels: 14.1 us -> 27.5 us
  local copies, waits for them, and re-layouts: 1.96 us -> 0 us
    pallas_call x1, Pallas kernels: 14.1 us -> 26.7 us  [body(): pl.pallas_call(functools.partial(kernel, n, tiles), out_shape=(pltpu.VMEM...]
    unnamed x3 -> x0, local copies, waits for them, and re-layouts: 1.96 us -> none
    pallas_call x0 -> x1, Pallas kernels: none -> 0.83 us  [body(): pl.pallas_call(write_out, out_shape=tuple((jax.ShapeDtypeStruct(r.shape,...]
where the time goes in v3:
time: 29 us; the launch traced here: 28.8 us
  Pallas kernels  27.5 us (95%)
  between operations  1.28 us (4%)
    pallas_call x1, Pallas kernels, body(): pl.pallas_call(functools.partial(kernel, n, tiles), out_shape=(pltpu.VMEM...  26.7 us
    pallas_call x1, Pallas kernels, body(): pl.pallas_call(write_out, out_shape=tuple((jax.ShapeDtypeStruct(r.shape,...  0.83 us

profile of v3, /device:TPU:1, one launch (start us, length us, event | category | flops | bytes accessed | tf_op | source)
XLA Modules:
  0.0 28.8 jit_solution(196585709677328886)
XLA Ops:
  1.3 26.7 %shard_map.85 = (bf16[1,64,4096]{2,1,0:T(8,128)(2,1)S(1)}, f32[1,2,1,64]{3,2,1,0:T(1,128)S(1)}, f32[1,8,512]{2,1,0:T(8,128)S(1)}) custom-call(s32[1]{0:T(128)S(6)} %copy.9.kf_hbm, s32[1,64]{1,0:T(1,128)} %off_hbm.1, bf16[32,64]{1,0:T(8,128)(2,1)} %constant.6.clone.first_hbm, bf16[64,96]{1,0:T(8,128)(2,1)} %constant.7.clone.second_hbm, ...), custom_call_target="tpu_custom_call" | custom-call | tf_op jit(solution)/shard_map/pallas_call | solution.py:451
  28.0 0.8 %shard_map.86 = (bf16[1,64,4096]{2,1,0:T(8,128)(2,1)}, f32[1,2,1,64]{3,2,1,0:T(1,128)}, f32[1,8,512]{2,1,0:T(8,128)}) custom-call(bf16[1,64,4096]{2,1,0:T(8,128)(2,1)S(1)} %get-tuple-element.6.a, f32[1,2,1,64]{3,2,1,0:T(1,128)S(1)} %get-tuple-element.7.b, f32[1,8,512]{2,1,0:T(8,128)S(1)} %get-tuple-element.8.c), custom_call_target="tpu_custom_call" | custom-call | tf_op jit(solution)/shard_map/pallas_call | solution.py:489

commit v4 on v2

--- a/solution.py
+++ b/solution.py
@@ -16,6 +16,7 @@
 BOX = 8
 LANES = 128
 PAD = 16
+U_PREP, U_VS, U_HS, U_V, U_H = 2, 4, 8, 1, 2
 MESH = pl.DeviceIdType.MESH
 F32 = jnp.float32
 BF16 = jnp.bfloat16
@@ -93,7 +94,7 @@
 def kernel(
     n, tiles, kf_hbm, off_hbm, first_hbm, second_hbm, column_hbm, x_hbm,
     obuf, field_ref, pyr_ref,
-    kf_ref, off_ref, first_ref, second_ref, column_ref, xext, coldct, expand, pool, compact, comm, shifted, vert, weights, normal, brecv, bsend, wsum,
+    kf_ref, off_ref, first_ref, second_ref, column_ref, xext, coldct, expand, pool, compact, comm, shifted, vert, weights, normal, brecv, bsend, wsum, tgroup,
     load_sem, table_sem, halo_ssem, halo_rsem, ssem, rsem, bssem, brsem,
 ):
     me = lax.axis_index("sec")
@@ -135,22 +136,59 @@
 
     fetches[0].wait()
     lane = lax.broadcasted_iota(jnp.int32, (PATCH, LANES), 1)
-    for term in range(3):
-        base = column_ref[term].astype(F32)
-        for p in range(group // PATCH):
-            coldct[term, p * PATCH : (p + 1) * PATCH, :] = jnp.where(
-                lane // KCOEF == p, base, 0.0
+
+    def build_columns(p, carry):
+        at = pl.ds(pl.multiple_of(p * PATCH, PATCH), PATCH)
+        for term in range(3):
+            coldct[term, at, :] = jnp.where(
+                lane // KCOEF == p, column_ref[term].astype(F32), 0.0
             ).astype(BF16)
-
+        return carry
+
+    lax.fori_loop(0, group // PATCH, build_columns, 0)
+
+    def build_squares(p, carry):
+        at = pl.ds(pl.multiple_of(p * LANES, LANES), LANES)
+        row_of = lax.broadcasted_iota(jnp.int32, (LANES, LANES), 0)
+        col_of = lax.broadcasted_iota(jnp.int32, (LANES, LANES), 1)
+        expand[:, at] = jnp.where(
+            row_of // KCOEF == (col_of + p * LANES) // PATCH, 1.0, 0.0
+        ).astype(BF16)
+        pool[at, :] = jnp.where((row_of + p * LANES) // BOX == col_of, 1.0, 0.0).astype(BF16)
+        return carry
+
+    lax.fori_loop(0, group // LANES, build_squares, 0)
+
+    def build_compact(p, carry):
+        at = pl.ds(pl.multiple_of(p * LANES, LANES), LANES)
+        shape = (LANES, compact.shape[1])
+        row_of = lax.broadcasted_iota(jnp.int32, shape, 0) + p * LANES
+        col_of = lax.broadcasted_iota(jnp.int32, shape, 1)
+        compact[at, :] = jnp.where(row_of // KCOEF == col_of, 1.0, 0.0).astype(BF16)
+        return carry
+
+    lax.fori_loop(0, compact.shape[0] // LANES, build_compact, 0)
+
+    def clear(r, carry):
+        at = pl.ds(pl.multiple_of(r * BOX, BOX), BOX)
+        vert[at, 0:LANES] = jnp.zeros((BOX, LANES), F32)
+        vert[at, LANES + cols : 2 * LANES + cols] = jnp.zeros((BOX, LANES), F32)
+        return carry
+
+    lax.fori_loop(0, (sums + rows) // BOX, clear, 0)
     fetches[1].wait()
     load.wait()
 
-    def first_dct(g):
-        part = dot(first_ref[...], xext[PAD : PAD + rows, g * group : (g + 1) * group])
-        return part[0:KCOEF] + part[KCOEF : 2 * KCOEF] + part[2 * KCOEF : 3 * KCOEF]
-
-    t_rows = [first_dct(g) for g in range(groups)]
-    t_group = jnp.concatenate(t_rows, axis=0)
+    def first_dct(g, carry):
+        at = pl.ds(pl.multiple_of(g * group, group), group)
+        part = dot(first_ref[...], xext[PAD : PAD + rows, at])
+        tgroup[0, pl.ds(pl.multiple_of(g * KCOEF, KCOEF), KCOEF), :] = (
+            part[0:KCOEF] + part[KCOEF : 2 * KCOEF] + part[2 * KCOEF : 3 * KCOEF]
+        )
+        return carry
+
+    lax.fori_loop(0, groups, first_dct, 0)
+    t_group = tgroup[0]
     parts = split(t_group, 2)
     size = t_group.shape[0]
     wide = dot(jnp.concatenate(parts, axis=0), coldct[0])
@@ -195,26 +233,22 @@
 
     @pl.when(mt == 0)
     def _():
-        xext[0:PAD, :] = jnp.zeros((PAD, cols), BF16)
+        def blank(v, carry):
+            xext[0:PAD, pl.ds(pl.multiple_of(v * group, group), group)] = jnp.zeros((PAD, group), BF16)
+            return carry
+
+        lax.fori_loop(0, groups, blank, 0)
 
     @pl.when(mt == tiles - 1)
     def _():
-        xext[PAD + rows : 2 * PAD + rows, :] = jnp.zeros((PAD, cols), BF16)
-
-    row_of = lax.broadcasted_iota(jnp.int32, (LANES, group), 0)
-    col_of = lax.broadcasted_iota(jnp.int32, (LANES, group), 1)
-    expand[...] = jnp.where(row_of // KCOEF == col_of // PATCH, 1.0, 0.0).astype(BF16)
-    row_of = lax.broadcasted_iota(jnp.int32, (group, LANES), 0)
-    col_of = lax.broadcasted_iota(jnp.int32, (group, LANES), 1)
-    pool[...] = jnp.where(row_of // BOX == col_of, 1.0, 0.0).astype(BF16)
-    row_of = lax.broadcasted_iota(jnp.int32, compact.shape, 0)
-    col_of = lax.broadcasted_iota(jnp.int32, compact.shape, 1)
-    compact[...] = jnp.where(row_of // KCOEF == col_of, 1.0, 0.0).astype(BF16)
-    zeros = jnp.zeros((vert.shape[0], LANES), F32)
-    vert[:, 0:LANES] = zeros
-    vert[:, LANES + cols : 2 * LANES + cols] = zeros
-
-    t_full = jnp.concatenate(t_rows, axis=1)
+        def blank(v, carry):
+            at = pl.ds(pl.multiple_of(v * group, group), group)
+            xext[PAD + rows : 2 * PAD + rows, at] = jnp.zeros((PAD, group), BF16)
+            return carry
+
+        lax.fori_loop(0, groups, blank, 0)
+
+    t_full = from_groups(tgroup[0], groups)
     where = lax.broadcasted_iota(jnp.int32, (KCOEF, cols), 1)
     after = jnp.where(where == cols - 1, 0.0, pltpu.roll(t_full, cols - 1, 1))
     before = jnp.where(where == 0, 0.0, pltpu.roll(t_full, 1, 1))
@@ -229,15 +263,19 @@
         to_next.wait_recv()
 
     fetches[2].wait()
-    ty_rows = []
-    for g in range(groups):
-        part = dot(second_ref[...], xext[:, g * group : (g + 1) * group])
-        ty_rows.append(part[0:KCOEF] + part[KCOEF : 2 * KCOEF] + part[2 * KCOEF : 3 * KCOEF])
+    def second_dct(g, carry):
+        at = pl.ds(pl.multiple_of(g * group, group), group)
+        part = dot(second_ref[...], xext[:, at])
+        tgroup[1, pl.ds(pl.multiple_of(g * KCOEF, KCOEF), KCOEF), :] = (
+            part[0:KCOEF] + part[KCOEF : 2 * KCOEF] + part[2 * KCOEF : 3 * KCOEF]
+        )
         for k in range(4):
-            at = 4 * KCOEF + k * sums
-            shifted[k, 0:sums, g * group : (g + 1) * group] = part[at : at + sums]
-    ty_group = jnp.concatenate(ty_rows, axis=0)
-
+            begin = 4 * KCOEF + k * sums
+            shifted[k, 0:sums, at] = part[begin : begin + sums]
+        return carry
+
+    lax.fori_loop(0, groups, second_dct, 0)
+    ty_group = tgroup[1]
     both = jnp.concatenate([tx_group, ty_group], axis=0)
     parts = split(both, 3)
     size = both.shape[0]
@@ -291,7 +329,7 @@
 
     @pl.when(me >= n // 2)
     def _():
-        lax.fori_loop(0, blocks, prepare, 0, unroll=4)
+        lax.fori_loop(0, blocks, prepare, 0, unroll=U_PREP)
 
     fetches[3].wait()
     fetches[4].wait()
@@ -343,12 +381,12 @@
             lanes = stacked(lane8, times)
             even = jnp.where(lanes >= 96, left, center)
             odd = jnp.where(lanes < 32, right, center)
-            even = pltpu.roll(even, (LANES - off_ref[0, 2 * v]) % LANES, 1)
-            odd = pltpu.roll(odd, (LANES - off_ref[0, 2 * v + 1]) % LANES, 1)
+            even = pltpu.roll(even, (LANES - off_ref[0, 2 * v]) & (LANES - 1), 1)
+            odd = pltpu.roll(odd, (LANES - off_ref[0, 2 * v + 1]) & (LANES - 1), 1)
             at = pl.ds(pl.multiple_of(v * LANES, LANES), LANES)
             total = None
             for k in range(-1, 3):
-                mine = ((lanes - k + LANES) % LANES) < PATCH
+                mine = ((lanes - k) & (LANES - 1)) < PATCH
                 both = jnp.where(mine, even, odd)
                 if k != 0:
                     both = pltpu.roll(both, (LANES - k) % LANES, 1)
@@ -365,8 +403,8 @@
     def store_rows(at, value):
         obuf[0, :, at] = value.astype(BF16)
 
-    lax.fori_loop(0, blocks, vertical(0, sums), 0, unroll=16)
-    lax.fori_loop(0, blocks, horizontal(0, sums, store_sums), 0, unroll=16)
+    lax.fori_loop(0, blocks, vertical(0, sums), 0, unroll=U_VS)
+    lax.fori_loop(0, blocks, horizontal(0, sums, store_sums), 0, unroll=U_HS)
     lhs = to_groups(wsum[...], group)
     size = lhs.shape[0]
     wide = dot(jnp.concatenate(split(lhs, 3), axis=0), pool[...])
@@ -387,10 +425,10 @@
 
     @pl.when(me < n // 2)
     def _():
-        lax.fori_loop(0, blocks, prepare, 0, unroll=4)
-
-    lax.fori_loop(0, blocks, vertical(sums, rows), 0, unroll=2)
-    lax.fori_loop(0, blocks, horizontal(sums, rows, store_rows), 0, unroll=4)
+        lax.fori_loop(0, blocks, prepare, 0, unroll=U_PREP)
+
+    lax.fori_loop(0, blocks, vertical(sums, rows), 0, unroll=U_V)
+    lax.fori_loop(0, blocks, horizontal(sums, rows, store_rows), 0, unroll=U_H)
 
     gxx, gxy, gyy, bx, by = narrow(normals + slants)
     gxx = gxx + REG
@@ -426,6 +464,17 @@
     @pl.when(mt > 0)
     def _():
         to_last.wait_send()
+
+
+def write_out(a, b, c, a_out, b_out, c_out, sem):
+    copies = [
+        pltpu.make_async_copy(source, target, sem.at[i])
+        for i, (source, target) in enumerate(((a, a_out), (b, b_out), (c, c_out)))
+    ]
+    for copy in copies:
+        copy.start()
+    for copy in copies:
+        copy.wait()
 
 
 def body(n, tiles, image, keyframe, offsets):
@@ -438,7 +487,7 @@
     vmem = pl.BlockSpec(memory_space=pltpu.VMEM)
     hbm = pl.BlockSpec(memory_space=pltpu.HBM)
     dma = pltpu.SemaphoreType.DMA
-    return pl.pallas_call(
+    results = pl.pallas_call(
         functools.partial(kernel, n, tiles),
         out_shape=(
             pltpu.VMEM(image.shape, BF16),
@@ -466,6 +515,7 @@
             pltpu.VMEM((WIN - 1, sums, cols // BOX), F32),
             pltpu.VMEM((sums, cols // BOX), F32),
             pltpu.VMEM((sums, cols), F32),
+            pltpu.VMEM((2, cols // group * KCOEF, group), F32),
             dma,
             dma((5,)),
             dma((2,)),
@@ -477,6 +527,13 @@
         ],
         compiler_params=pltpu.CompilerParams(collective_id=0, has_side_effects=True),
     )(keyframe, offsets, jnp.asarray(first), jnp.asarray(second), jnp.asarray(column), image)
+    return pl.pallas_call(
+        write_out,
+        out_shape=tuple(jax.ShapeDtypeStruct(r.shape, r.dtype) for r in results),
+        in_specs=[vmem] * 3,
+        out_specs=(hbm,) * 3,
+        scratch_shapes=[dma((3,))],
+    )(*[pltpu.with_memory_space_constraint(r, pltpu.VMEM) for r in results])
 
 
 def solution(mesh):

time: 17.5 us -> 17.5 us (level)
  local copies, waits for them, and re-layouts: 1.96 us -> 0 us
  Pallas kernels: 14.1 us -> 16 us
    unnamed x3 -> x0, local copies, waits for them, and re-layouts: 1.96 us -> none
    pallas_call x1, Pallas kernels: 14.1 us -> 15.2 us  [body(): pl.pallas_call(functools.partial(kernel, n, tiles), out_shape=(pltpu.VMEM...]
    pallas_call x0 -> x1, Pallas kernels: none -> 0.83 us  [body(): pl.pallas_call(write_out, out_shape=tuple((jax.ShapeDtypeStruct(r.shape,...]
where the time goes in v4:
time: 17.5 us; the launch traced here: 17.3 us
  Pallas kernels  16 us (91%)
  between operations  1.28 us (7%)
    pallas_call x1, Pallas kernels, body(): pl.pallas_call(functools.partial(kernel, n, tiles), out_shape=(pltpu.VMEM...  15.2 us
    pallas_call x1, Pallas kernels, body(): pl.pallas_call(write_out, out_shape=tuple((jax.ShapeDtypeStruct(r.shape,...  0.83 us

profile of v4, /device:TPU:1, one launch (start us, length us, event | category | flops | bytes accessed | tf_op | source)
XLA Modules:
  0.0 17.3 jit_solution(11763332649540564368)
XLA Ops:
  1.3 15.2 %shard_map.85 = (bf16[1,64,4096]{2,1,0:T(8,128)(2,1)S(1)}, f32[1,2,1,64]{3,2,1,0:T(1,128)S(1)}, f32[1,8,512]{2,1,0:T(8,128)S(1)}) custom-call(s32[1]{0:T(128)S(6)} %copy.9.kf_hbm, s32[1,64]{1,0:T(1,128)} %off_hbm.1, bf16[32,64]{1,0:T(8,128)(2,1)} %constant.6.clone.first_hbm, bf16[64,96]{1,0:T(8,128)(2,1)} %constant.7.clone.second_hbm, ...), custom_call_target="tpu_custom_call" | custom-call | tf_op jit(solution)/shard_map/pallas_call | solution.py:490
  16.5 0.8 %shard_map.86 = (bf16[1,64,4096]{2,1,0:T(8,128)(2,1)}, f32[1,2,1,64]{3,2,1,0:T(1,128)}, f32[1,8,512]{2,1,0:T(8,128)}) custom-call(bf16[1,64,4096]{2,1,0:T(8,128)(2,1)S(1)} %get-tuple-element.6.a, f32[1,2,1,64]{3,2,1,0:T(1,128)S(1)} %get-tuple-element.7.b, f32[1,8,512]{2,1,0:T(8,128)S(1)} %get-tuple-element.8.c), custom_call_target="tpu_custom_call" | custom-call | tf_op jit(solution)/shard_map/pallas_call | solution.py:530

commit v5 on v4

--- a/solution.py
+++ b/solution.py
@@ -16,7 +16,7 @@
 BOX = 8
 LANES = 128
 PAD = 16
-U_PREP, U_VS, U_HS, U_V, U_H = 2, 4, 8, 1, 2
+U_HS, U_H = 32, 4
 MESH = pl.DeviceIdType.MESH
 F32 = jnp.float32
 BF16 = jnp.bfloat16
@@ -175,7 +175,7 @@
         vert[at, LANES + cols : 2 * LANES + cols] = jnp.zeros((BOX, LANES), F32)
         return carry
 
-    lax.fori_loop(0, (sums + rows) // BOX, clear, 0)
+    lax.fori_loop(0, rows // BOX, clear, 0)
     fetches[1].wait()
     load.wait()
 
@@ -318,19 +318,6 @@
     normal[2] = gyy
     normal[3] = 1.0 / (gxx * gyy - gxy * gxy)
 
-    def prepare(v, carry):
-        at = pl.ds(pl.multiple_of(v * LANES, LANES), LANES)
-        block = xext[:, at].astype(F32)
-        height = block.shape[0]
-        for k in range(4):
-            moved = block if k == 1 else pltpu.roll(block, (height - (k - 1)) % height, 0)
-            shifted[k, sums : sums + rows, at] = moved[PAD : PAD + rows]
-        return carry
-
-    @pl.when(me >= n // 2)
-    def _():
-        lax.fori_loop(0, blocks, prepare, 0, unroll=U_PREP)
-
     fetches[3].wait()
     fetches[4].wait()
 
@@ -357,37 +344,50 @@
 
     lane8 = lax.broadcasted_iota(jnp.int32, (BOX, LANES), 1)
 
-    def vertical(low, count):
+    def block_at(v):
+        return pl.ds(pl.multiple_of(v * LANES, LANES), LANES)
+
+    def sums_at(at):
+        return [shifted[k, :, at] for k in range(4)]
+
+    def rows_at(at):
+        whole = xext[:, at].astype(F32)
+        height = whole.shape[0]
+        return [
+            (whole if k == 0 else pltpu.roll(whole, (height - k) % height, 0))[PAD : PAD + rows]
+            for k in range(-1, 3)
+        ]
+
+    def vertical(count, fetch):
         times = count // BOX
 
         def run(v, carry):
-            at = pl.ds(pl.multiple_of(v * LANES, LANES), LANES)
-            total = stacked(weights[4, :, at], times) * shifted[0, low : low + count, at]
-            for k in range(1, 4):
-                total = total + stacked(weights[4 + k, :, at], times) * shifted[k, low : low + count, at]
-            vert[low : low + count, pl.ds(pl.multiple_of((v + 1) * LANES, LANES), LANES)] = total
+            at = block_at(jnp.minimum(v, blocks - 1))
+            total = None
+            for k, part in enumerate(fetch(at)):
+                term = stacked(weights[4 + k, :, at], times) * part
+                total = term if total is None else total + term
+            vert[0:count, block_at(jnp.where(v < blocks, v + 1, blocks + 2))] = total
             return carry
 
         return run
 
-    def horizontal(low, count, store):
+    def horizontal(count, store):
         times = count // BOX
 
         def run(v, carry):
-            span = slice(low, low + count)
-            left = vert[span, pl.ds(pl.multiple_of(v * LANES, LANES), LANES)]
-            center = vert[span, pl.ds(pl.multiple_of((v + 1) * LANES, LANES), LANES)]
-            right = vert[span, pl.ds(pl.multiple_of((v + 2) * LANES, LANES), LANES)]
+            left = vert[0:count, block_at(v)]
+            center = vert[0:count, block_at(v + 1)]
+            right = vert[0:count, block_at(v + 2)]
             lanes = stacked(lane8, times)
             even = jnp.where(lanes >= 96, left, center)
             odd = jnp.where(lanes < 32, right, center)
             even = pltpu.roll(even, (LANES - off_ref[0, 2 * v]) & (LANES - 1), 1)
             odd = pltpu.roll(odd, (LANES - off_ref[0, 2 * v + 1]) & (LANES - 1), 1)
-            at = pl.ds(pl.multiple_of(v * LANES, LANES), LANES)
+            at = block_at(v)
             total = None
             for k in range(-1, 3):
-                mine = ((lanes - k) & (LANES - 1)) < PATCH
-                both = jnp.where(mine, even, odd)
+                both = jnp.where(((lanes - k) & (LANES - 1)) < PATCH, even, odd)
                 if k != 0:
                     both = pltpu.roll(both, (LANES - k) % LANES, 1)
                 term = stacked(weights[k + 1, :, at], times) * both
@@ -397,14 +397,25 @@
 
         return run
 
+    def warp(count, fetch, store, unroll):
+        down = vertical(count, fetch)
+        across = horizontal(count, store)
+
+        def run(v, carry):
+            across(v, carry)
+            return down(v + 2, carry)
+
+        lax.fori_loop(0, 2, down, 0)
+        lax.fori_loop(0, blocks, run, 0, unroll=unroll)
+
     def store_sums(at, value):
         wsum[:, at] = value
 
     def store_rows(at, value):
         obuf[0, :, at] = value.astype(BF16)
 
-    lax.fori_loop(0, blocks, vertical(0, sums), 0, unroll=U_VS)
-    lax.fori_loop(0, blocks, horizontal(0, sums, store_sums), 0, unroll=U_HS)
+    lax.fori_loop(0, blocks, vertical(sums, sums_at), 0, unroll=8)
+    lax.fori_loop(0, blocks, horizontal(sums, store_sums), 0, unroll=U_HS)
     lhs = to_groups(wsum[...], group)
     size = lhs.shape[0]
     wide = dot(jnp.concatenate(split(lhs, 3), axis=0), pool[...])
@@ -423,12 +434,7 @@
         def _():
             block_copy(d).start()
 
-    @pl.when(me < n // 2)
-    def _():
-        lax.fori_loop(0, blocks, prepare, 0, unroll=U_PREP)
-
-    lax.fori_loop(0, blocks, vertical(sums, rows), 0, unroll=U_V)
-    lax.fori_loop(0, blocks, horizontal(sums, rows, store_rows), 0, unroll=U_H)
+    warp(rows, rows_at, store_rows, U_H)
 
     gxx, gxy, gyy, bx, by = narrow(normals + slants)
     gxx = gxx + REG
@@ -508,8 +514,8 @@
             pltpu.VMEM((group, LANES), BF16),
             pltpu.VMEM((coefs, cols // PATCH), BF16),
             pltpu.VMEM((n, KCOEF, coefs), BF16),
-            pltpu.VMEM((4, sums + rows, cols), F32),
-            pltpu.VMEM((sums + rows, cols + 2 * LANES), F32),
+            pltpu.VMEM((4, sums, cols), F32),
+            pltpu.VMEM((rows, cols + 3 * LANES), F32),
             pltpu.VMEM((8, KCOEF, cols), F32),
             pltpu.VMEM((4, KCOEF, cols), F32),
             pltpu.VMEM((WIN - 1, sums, cols // BOX), F32),

time: 17.5 us -> 15.3 us (0.87)
  Pallas kernels: 16 us -> 13.9 us
    pallas_call x1, Pallas kernels: 15.2 us -> 13.1 us  [body(): pl.pallas_call(functools.partial(kernel, n, tiles), out_shape=(pltpu.VMEM...]
where the time goes in v5:
time: 15.3 us; the launch traced here: 15.2 us
  Pallas kernels  13.9 us (91%)
  between operations  1.28 us (8%)
    pallas_call x1, Pallas kernels, body(): pl.pallas_call(functools.partial(kernel, n, tiles), out_shape=(pltpu.VMEM...  13.1 us
    pallas_call x1, Pallas kernels, body(): pl.pallas_call(write_out, out_shape=tuple((jax.ShapeDtypeStruct(r.shape,...  0.83 us

profile of v5, /device:TPU:1, one launch (start us, length us, event | category | flops | bytes accessed | tf_op | source)
XLA Modules:
  0.0 15.2 jit_solution(12796110650860812375)
XLA Ops:
  1.3 13.1 %shard_map.85 = (bf16[1,64,4096]{2,1,0:T(8,128)(2,1)S(1)}, f32[1,2,1,64]{3,2,1,0:T(1,128)S(1)}, f32[1,8,512]{2,1,0:T(8,128)S(1)}) custom-call(s32[1]{0:T(128)S(6)} %copy.9.kf_hbm, s32[1,64]{1,0:T(1,128)} %off_hbm.1, bf16[32,64]{1,0:T(8,128)(2,1)} %constant.6.clone.first_hbm, bf16[64,96]{1,0:T(8,128)(2,1)} %constant.7.clone.second_hbm, ...), custom_call_target="tpu_custom_call" | custom-call | tf_op jit(solution)/shard_map/pallas_call | solution.py:496
  14.4 0.8 %shard_map.86 = (bf16[1,64,4096]{2,1,0:T(8,128)(2,1)}, f32[1,2,1,64]{3,2,1,0:T(1,128)}, f32[1,8,512]{2,1,0:T(8,128)}) custom-call(bf16[1,64,4096]{2,1,0:T(8,128)(2,1)S(1)} %get-tuple-element.6.a, f32[1,2,1,64]{3,2,1,0:T(1,128)S(1)} %get-tuple-element.7.b, f32[1,8,512]{2,1,0:T(8,128)S(1)} %get-tuple-element.8.c), custom_call_target="tpu_custom_call" | custom-call | tf_op jit(solution)/shard_map/pallas_call | solution.py:536
